TPU v7x, 512 devices: a whole 4x8x8 slice. The times are simulated.
512 devices in a mesh: angle: 8 (over x, core), gx: 16 (over y, z_lo), gy: 4 (over z_hi).
Axes of the slice: x: 4, y: 8, z: 8 (z_hi: 4, z_lo: 2; z = z_hi * 2 + z_lo), core: 2. Of those that a mesh axis runs over, the one named last changes fastest.
Arguments:
- forward_fields: float32 [8, 12, 128, 64, 128], P('angle', None, 'gx', 'gy'), may hold values from -6 to 6
- adjoint_fields: float32 [8, 12, 128, 64, 128], P('angle', None, 'gx', 'gy'), may hold values from -6 to 6
- forward_spectrum: float32 [8, 6, 128, 64, 128], P('angle', None, 'gx', 'gy'), may hold values from -6 to 6
- adjoint_spectrum: float32 [8, 6, 128, 64, 128], P('angle', None, 'gx', 'gy'), may hold values from -6 to 6
- permittivity: float32 [128, 64, 128], P('gx', 'gy'), may hold values from 1 to 12
- phase_table: float32 [8, 2], replicated, may hold values from -3.140625 to 3.140625
- angle_index: int32 [8], P('angle'), may hold values from 0 to 7, each once
- design_tiles: int32 [16], replicated, may hold values from 0 to 63, as said below
Outputs:
- forward_transform: float32 [8, 6, 128, 64, 128], P('angle', None, 'gx', 'gy')
- adjoint_transform: float32 [8, 6, 128, 64, 128], P('angle', None, 'gx', 'gy')
- gradient: float32 [128, 64, 128], P('gx', 'gy', 'angle')
Inputs may be any that keep to these rules, and one draw needn't show every extreme that they name: `angle_index`: every row of phase_table is used by exactly one angle. `design_tiles`: 16 distinct tile numbers; tiles 0 and 63 are always among them.
All inputs are finite; a program needn't handle non-finite values.
Results may differ from a plain program's by a relative error of at most 0.0001.
Values sent between devices are 32-bit elements; how exact they have to be, the bound alone decides.
A program may use at most 64 MiB of HBM per device.

v0:
```python
import math
import jax
import jax.numpy as jnp
from jax import lax
from jax.sharding import PartitionSpec as P

STEPS = 3
courant = 0.5
omega_step = 0.7


def from_behind(value, axis, steps):
    count = lax.axis_size(axis)
    pairs = [(source, (source + steps) % count) for source in range(count)]
    return lax.ppermute(value, axis, pairs)


def rotate_runs(pair, cosine, sine):
    sine_full = sine.reshape((2,) + (1,) * (pair.ndim - 2))
    real_part = pair[:, 0]
    imag_part = pair[:, 1]
    return jnp.stack(
        [real_part * cosine - imag_part * sine_full, real_part * sine_full + imag_part * cosine],
        axis=1,
    )


def next_depth(field):
    return jnp.concatenate([field[..., 1:], jnp.zeros_like(field[..., :1])], axis=-1)


def prev_depth(field):
    return jnp.concatenate([jnp.zeros_like(field[..., :1]), field[..., :-1]], axis=-1)


def curl_forward(efield, phases):
    cos_x, sine_x, cos_y, sine_y = phases
    place_x = lax.axis_index("gx")
    place_y = lax.axis_index("gy")
    last_x = lax.axis_size("gx") - 1
    last_y = lax.axis_size("gy") - 1
    send_x = efield[:, :, 1:3, 0]
    got_x = from_behind(send_x, "gx", -1)
    got_x = jnp.where(place_x == last_x, rotate_runs(got_x, cos_x, sine_x), got_x)
    send_y = jnp.stack([efield[:, :, 0, :, 0], efield[:, :, 2, :, 0]], axis=2)
    got_y = from_behind(send_y, "gy", -1)
    got_y = jnp.where(place_y == last_y, rotate_runs(got_y, cos_y, sine_y), got_y)
    comp_x = efield[:, :, 0]
    comp_y = efield[:, :, 1]
    comp_z = efield[:, :, 2]
    dz_dy = jnp.concatenate([comp_z[:, :, :, 1:], got_y[:, :, 1][:, :, :, None]], axis=3) - comp_z
    dy_dz = next_depth(comp_y) - comp_y
    dx_dz = next_depth(comp_x) - comp_x
    dz_dx = jnp.concatenate([comp_z[:, :, 1:], got_x[:, :, 1][:, :, None]], axis=2) - comp_z
    dy_dx = jnp.concatenate([comp_y[:, :, 1:], got_x[:, :, 0][:, :, None]], axis=2) - comp_y
    dx_dy = jnp.concatenate([comp_x[:, :, :, 1:], got_y[:, :, 0][:, :, :, None]], axis=3) - comp_x
    return jnp.stack([dz_dy - dy_dz, dx_dz - dz_dx, dy_dx - dx_dy], axis=2)


def curl_backward(hfield, phases):
    cos_x, sine_x, cos_y, sine_y = phases
    place_x = lax.axis_index("gx")
    place_y = lax.axis_index("gy")
    send_x = hfield[:, :, 1:3, -1]
    got_x = from_behind(send_x, "gx", 1)
    got_x = jnp.where(place_x == 0, rotate_runs(got_x, cos_x, -sine_x), got_x)
    send_y = jnp.stack([hfield[:, :, 0, :, -1], hfield[:, :, 2, :, -1]], axis=2)
    got_y = from_behind(send_y, "gy", 1)
    got_y = jnp.where(place_y == 0, rotate_runs(got_y, cos_y, -sine_y), got_y)
    comp_x = hfield[:, :, 0]
    comp_y = hfield[:, :, 1]
    comp_z = hfield[:, :, 2]
    hz_below_y = jnp.concatenate([got_y[:, :, 1][:, :, :, None], comp_z[:, :, :, :-1]], axis=3)
    hx_below_y = jnp.concatenate([got_y[:, :, 0][:, :, :, None], comp_x[:, :, :, :-1]], axis=3)
    hz_below_x = jnp.concatenate([got_x[:, :, 1][:, :, None], comp_z[:, :, :-1]], axis=2)
    hy_below_x = jnp.concatenate([got_x[:, :, 0][:, :, None], comp_y[:, :, :-1]], axis=2)
    first = comp_z - hz_below_y - (comp_y - prev_depth(comp_y))
    second = comp_x - prev_depth(comp_x) - (comp_z - hz_below_x)
    third = comp_y - hy_below_x - (comp_x - hx_below_y)
    return jnp.stack([first, second, third], axis=2)


def shards(
    forward_fields,
    adjoint_fields,
    forward_spectrum,
    adjoint_spectrum,
    permittivity,
    phase_table,
    angle_index,
    design_tiles,
):
    cells = forward_fields.shape[2:]
    fields = jnp.concatenate([forward_fields, adjoint_fields], axis=0)
    spectrum = jnp.concatenate([forward_spectrum, adjoint_spectrum], axis=0).reshape(
        (2, 2, 3) + cells
    )
    table_rows = phase_table.shape[0]
    picked = (jnp.arange(table_rows) == angle_index[0]).astype(jnp.float32)
    angle_x = jnp.sum(picked * phase_table[:, 0])
    angle_y = jnp.sum(picked * phase_table[:, 1])
    run_sign = jnp.array([1.0, -1.0], jnp.float32)
    efield = fields[:, 0:6].reshape((2, 2, 3) + cells)
    hfield = fields[:, 6:12].reshape((2, 2, 3) + cells)
    phases = (
        jnp.cos(angle_x),
        run_sign * jnp.sin(angle_x),
        jnp.cos(angle_y),
        run_sign * jnp.sin(angle_y),
    )
    coef = courant / permittivity
    for step in range(STEPS):
        hfield = hfield - courant * curl_forward(efield, phases)
        efield = efield + coef * curl_backward(hfield, phases)
        theta = omega_step * (step + 1)
        spectrum = spectrum + rotate_runs(
            efield, math.cos(theta), jnp.full((2,), math.sin(theta), jnp.float32)
        )
    local_term = jnp.sum(spectrum[0, 0] * spectrum[1, 0] - spectrum[0, 1] * spectrum[1, 1], axis=0)
    own_tile = lax.axis_index("gx") * lax.axis_size("gy") + lax.axis_index("gy")
    chosen = jnp.any(design_tiles == own_tile)
    local_term = jnp.where(chosen, local_term, jnp.zeros_like(local_term))
    groups = lax.axis_size("angle")
    whole = lax.psum(local_term, "angle")
    share = whole.shape[2] // groups
    summed = lax.dynamic_slice_in_dim(whole, lax.axis_index("angle") * share, share, 2)
    gradient = summed * (1.0 / groups)
    forward_out = spectrum[0].reshape((1, 6) + cells)
    adjoint_out = spectrum[1].reshape((1, 6) + cells)
    return (forward_out, adjoint_out, gradient)


def solution(mesh):
    in_specs = (
        P("angle", None, "gx", "gy", None),
        P("angle", None, "gx", "gy", None),
        P("angle", None, "gx", "gy", None),
        P("angle", None, "gx", "gy", None),
        P("gx", "gy", None),
        P(),
        P("angle"),
        P(),
    )
    out_specs = (
        P("angle", None, "gx", "gy", None),
        P("angle", None, "gx", "gy", None),
        P("gx", "gy", "angle"),
    )
    return jax.shard_map(shards, mesh=mesh, in_specs=in_specs, out_specs=out_specs, check_vma=False)
```

profile of v0, /device:TPU:8, one launch (start us, length us, event | category | flops | bytes accessed | tf_op | source)
XLA Modules:
  0.0 201.6 jit_solution(371373391882974185)
XLA Ops:
  9.4 11.1 %collective-permute-start = (f32[2,2,2,8,128]{4,1,0,3,2:T(2,128)}, f32[2,2,2,8,128]{4,1,0,3,2:T(2,128)}, u32[]{:S(2)}, u32[]{:S(2)}) collective-permute-start(f32[2,2,2,8,128]{4,1,0,3,2:T(2,128)} %pad_maximum_fusion.1), channel_id=1, source_target_pairs={{0,3},{1,0},{2,1},{3,2},{4,7},{5,4},{6,5},{7,6},{8,11},{9,8},{10,9... | collective-permute-start | bytes 98312 | tf_op jit(solution)/shard_map/ppermute | solution.py:15
  21.8 3.3 %collective-permute-start.1 = (f32[2,2,2,16,128]{4,1,0,3,2:T(2,128)}, f32[2,2,2,16,128]{4,1,0,3,2:T(2,128)S(1)}, u32[]{:S(2)}, u32[]{:S(2)}) collective-permute-start(f32[2,2,2,16,128]{4,1,0,3,2:T(2,128)} %slice_bitcast_fusion.25), channel_id=1, source_target_pairs={{0,60},{4,0},{8,4},{12,8},{16,12},{20,16},{24,20},{28,24},{32,28},... | collective-permute-start | bytes 196616 | tf_op jit(solution)/shard_map/ppermute | solution.py:15
  35.7 2.0 %slice.554 = f32[2,2,8,16,127]{4,1,0,3,2:T(2,128)} slice(f32[2,2,8,16,128]{4,1,0,3,2:T(2,128)} %copy-done.4), slice={[0:2], [0:2], [0:8], [0:16], [1:128]} | slice | bytes 520192 | tf_op jit(solution)/shard_map/slice | solution.py:29
  37.8 1.7 slice.547
  39.4 1.6 slice.557
  44.2 1.4 fusion.11
  47.5 2.6 %collective-permute-start.3 = (f32[2,2,2,16,128]{4,1,0,3,2:T(2,128)S(1)}, f32[2,2,2,16,128]{4,1,0,3,2:T(2,128)S(1)}, u32[]{:S(2)}, u32[]{:S(2)}) collective-permute-start(f32[2,2,2,16,128]{4,1,0,3,2:T(2,128)S(1)} %slice_bitcast_fusion.24), channel_id=1, source_target_pairs={{0,4},{4,8},{8,12},{12,16},{16,20},{20,24},{24,28},{28,32},{32,36}... | collective-permute-start | bytes 196616 | tf_op jit(solution)/shard_map/ppermute | solution.py:15
  50.1 1.9 collective-permute-start.2
  52.1 5.9 %collective-permute-done.2 = f32[2,2,2,8,128]{4,1,0,3,2:T(2,128)S(1)} collective-permute-done((f32[2,2,2,8,128]{4,1,0,3,2:T(2,128)S(1)}, f32[2,2,2,8,128]{4,1,0,3,2:T(2,128)S(1)}, u32[]{:S(2)}, u32[]{:S(2)}) %collective-permute-start.2) | collective-permute-done | bytes 32800 | tf_op jit(solution)/shard_map/ppermute | solution.py:15
  61.9 1.9 collective-permute-start.4
  64.6 4.5 %collective-permute-start.5 = (f32[2,2,2,16,128]{4,1,0,3,2:T(2,128)S(1)}, f32[2,2,2,16,128]{4,1,0,3,2:T(2,128)S(1)}, u32[]{:S(2)}, u32[]{:S(2)}) collective-permute-start(f32[2,2,2,16,128]{4,1,0,3,2:T(2,128)S(1)} %slice_bitcast_fusion.23), channel_id=1, source_target_pairs={{0,60},{4,0},{8,4},{12,8},{16,12},{20,16},{24,20},{28,24},{32,28},... | collective-permute-start | bytes 196616 | tf_op jit(solution)/shard_map/ppermute | solution.py:15
  69.2 1.9 collective-permute-done.5
  74.2 4.8 %collective-permute-start.6 = (f32[2,2,2,8,128]{4,3,2,1,0:T(8,128)S(1)}, f32[2,2,2,8,128]{4,3,2,1,0:T(8,128)S(1)}, u32[]{:S(2)}, u32[]{:S(2)}) collective-permute-start(f32[2,2,2,8,128]{4,3,2,1,0:T(8,128)S(1)} %pad_maximum_fusion.4), channel_id=1, source_target_pairs={{0,1},{1,2},{2,3},{3,0},{4,5},{5,6},{6,7},{7,4},{8,9},{9,10},{10,1... | collective-permute-start | bytes 98312 | tf_op jit(solution)/shard_map/ppermute | solution.py:15
  79.0 4.8 %collective-permute-start.7 = (f32[2,2,2,16,128]{4,1,0,3,2:T(2,128)S(1)}, f32[2,2,2,16,128]{4,1,0,3,2:T(2,128)S(1)}, u32[]{:S(2)}, u32[]{:S(2)}) collective-permute-start(f32[2,2,2,16,128]{4,1,0,3,2:T(2,128)S(1)} %bitcast.365), channel_id=1, source_target_pairs={{0,4},{4,8},{8,12},{12,16},{16,20},{20,24},{24,28},{28,32},{32,36}... | collective-permute-start | bytes 196616 | tf_op jit(solution)/shard_map/ppermute | solution.py:15
  84.3 1.7 collective-permute-done.7
  89.9 3.1 %collective-permute-start.8 = (f32[2,2,2,8,128]{4,1,0,3,2:T(2,128)S(1)}, f32[2,2,2,8,128]{4,1,0,3,2:T(2,128)S(1)}, u32[]{:S(2)}, u32[]{:S(2)}) collective-permute-start(f32[2,2,2,8,128]{4,1,0,3,2:T(2,128)S(1)} %pad_maximum_fusion.5), channel_id=1, source_target_pairs={{0,3},{1,0},{2,1},{3,2},{4,7},{5,4},{6,5},{7,6},{8,11},{9,8},{10,9... | collective-permute-start | bytes 98312 | tf_op jit(solution)/shard_map/ppermute | solution.py:15
  93.7 4.7 %collective-permute-start.9 = (f32[2,2,2,16,128]{4,1,0,3,2:T(2,128)S(1)}, f32[2,2,2,16,128]{4,1,0,3,2:T(2,128)S(1)}, u32[]{:S(2)}, u32[]{:S(2)}) collective-permute-start(f32[2,2,2,16,128]{4,1,0,3,2:T(2,128)S(1)} %slice_bitcast_fusion.22), channel_id=1, source_target_pairs={{0,60},{4,0},{8,4},{12,8},{16,12},{20,16},{24,20},{28,24},{32,28},... | collective-permute-start | bytes 196616 | tf_op jit(solution)/shard_map/ppermute | solution.py:15
  98.6 1.7 collective-permute-done.9
  102.9 3.6 %collective-permute-start.10 = (f32[2,2,2,8,128]{4,3,2,1,0:T(8,128)S(1)}, f32[2,2,2,8,128]{4,3,2,1,0:T(8,128)S(1)}, u32[]{:S(2)}, u32[]{:S(2)}) collective-permute-start(f32[2,2,2,8,128]{4,3,2,1,0:T(8,128)S(1)} %copy.222), channel_id=1, source_target_pairs={{0,1},{1,2},{2,3},{3,0},{4,5},{5,6},{6,7},{7,4},{8,9},{9,10},{10,1... | collective-permute-start | bytes 98312 | tf_op jit(solution)/shard_map/ppermute | solution.py:15
  106.5 4.6 %collective-permute-start.11 = (f32[2,2,2,16,128]{4,1,0,3,2:T(2,128)S(1)}, f32[2,2,2,16,128]{4,1,0,3,2:T(2,128)S(1)}, u32[]{:S(2)}, u32[]{:S(2)}) collective-permute-start(f32[2,2,2,16,128]{4,1,0,3,2:T(2,128)S(1)} %bitcast.364), channel_id=1, source_target_pairs={{0,4},{4,8},{8,12},{12,16},{16,20},{20,24},{24,28},{28,32},{32,36}... | collective-permute-start | bytes 196616 | tf_op jit(solution)/shard_map/ppermute | solution.py:15
  111.6 3.5 %collective-permute-done.11 = f32[2,2,2,16,128]{4,1,0,3,2:T(2,128)S(1)} collective-permute-done((f32[2,2,2,16,128]{4,1,0,3,2:T(2,128)S(1)}, f32[2,2,2,16,128]{4,1,0,3,2:T(2,128)S(1)}, u32[]{:S(2)}, u32[]{:S(2)}) %collective-permute-start.11) | collective-permute-done | bytes 65568 | tf_op jit(solution)/shard_map/ppermute | solution.py:15
  118.9 2.4 %fusion.3 = f32[2,2,3,8,16,128]{5,1,0,4,2,3:T(2,128)S(1)} fusion(f32[2,1,3,8,16,128]{5,1,0,4,2,3:T(1,128)S(1)} %get-tuple-element.40, f32[2,1,3,8,16,128]{5,1,0,4,2,3:T(1,128)S(1)} %get-tuple-element.39, f32[2,1,3,8,16,128]{5,1,0,4,2,3:T(1,128)S(1)} %get-tuple-element.25, f32[2,1,3,8,16,128]{5,1,0,4,2,3:T(1,128)S(1)} %get-tuple-element.24, ...), kind=kLoop, calls=%fused_computation.7 | loop fusion | flops 1179648 | bytes 3932160 | tf_op jit(solution)/shard_map/add | solution.py:116
  125.1 68.1 %all-reduce.14.cloned.1.call-done = f32[8,16,128]{2,1,0:T(8,128)} async-done(((f32[8,16,128]{2,1,0:T(8,128)}), f32[8,16,128]{2,1,0:T(8,128)}) %all-reduce.14.cloned.1.call-update) | async-done | bytes 65552 | tf_op jit(solution)/shard_map/psum | solution.py:124
  193.2 1.6 dynamic-slice_multiply_fusion
  (168 shorter events, 38.7 us)
Async XLA Ops:
  7.2 1.4 copy-start.9
  7.2 186.1 %all-reduce.14.cloned.1.call-start = ((), (), s32[]{:S(2)}) async-start(), calls=%async_computation | async-start | bytes 131072 | tf_op jit(solution)/shard_map/psum | solution.py:124
  9.4 16.4 %copy-start.10 = (f32[8,2]{0,1:T(2,128)S(1)}, f32[8,2]{0,1:T(2,128)}, u32[]{:S(2)}) copy-start(f32[8,2]{0,1:T(2,128)} %param.14) | copy-start | bytes 196
  9.4 32.7 %collective-permute-start = (f32[2,2,2,8,128]{4,1,0,3,2:T(2,128)}, f32[2,2,2,8,128]{4,1,0,3,2:T(2,128)}, u32[]{:S(2)}, u32[]{:S(2)}) collective-permute-start(f32[2,2,2,8,128]{4,1,0,3,2:T(2,128)} %pad_maximum_fusion.1), channel_id=1, source_target_pairs={{0,3},{1,0},{2,1},{3,2},{4,7},{5,4},{6,5},{7,6},{8,11},{9,8},{10,9... | collective-permute-start | bytes 98312 | tf_op jit(solution)/shard_map/ppermute | solution.py:15
  21.8 22.2 %collective-permute-start.1 = (f32[2,2,2,16,128]{4,1,0,3,2:T(2,128)}, f32[2,2,2,16,128]{4,1,0,3,2:T(2,128)S(1)}, u32[]{:S(2)}, u32[]{:S(2)}) collective-permute-start(f32[2,2,2,16,128]{4,1,0,3,2:T(2,128)} %slice_bitcast_fusion.25), channel_id=1, source_target_pairs={{0,60},{4,0},{8,4},{12,8},{16,12},{20,16},{24,20},{28,24},{32,28},... | collective-permute-start | bytes 196616 | tf_op jit(solution)/shard_map/ppermute | solution.py:15
  25.1 5.3 %copy-start = (f32[2,2,1,8,16,128]{5,4,3,2,1,0:T(8,128)}, f32[2,2,1,8,16,128]{5,4,3,2,1,0:T(8,128)S(1)}, u32[]{:S(2)}) copy-start(f32[2,2,1,8,16,128]{5,4,3,2,1,0:T(8,128)S(1)} %get-tuple-element.49) | copy-start | bytes 786436
  25.1 5.2 %copy-start.2 = (f32[2,2,8,16,128]{4,1,0,3,2:T(2,128)}, f32[2,2,8,16,128]{4,1,0,3,2:T(2,128)S(1)}, u32[]{:S(2)}) copy-start(f32[2,2,8,16,128]{4,1,0,3,2:T(2,128)S(1)} %slice_bitcast_fusion.21) | copy-start | bytes 786436
  28.9 1.5 copy-start.4
  35.7 5.3 %copy-start.3 = (f32[2,2,8,16,128]{4,1,0,3,2:T(2,128)S(1)}, f32[2,2,8,16,128]{4,1,0,3,2:T(2,128)}, u32[]{:S(2)}) copy-start(f32[2,2,8,16,128]{4,1,0,3,2:T(2,128)} %copy-done.2) | copy-start | bytes 786436
  42.1 3.5 %copy-start.1 = (f32[2,2,1,8,16,128]{5,4,3,2,1,0:T(8,128)S(1)}, f32[2,2,1,8,16,128]{5,4,3,2,1,0:T(8,128)}, u32[]{:S(2)}) copy-start(f32[2,2,1,8,16,128]{5,4,3,2,1,0:T(8,128)} %copy-done) | copy-start | bytes 786436
  42.1 3.5 %copy-start.5 = (f32[2,2,8,16,127]{4,1,0,3,2:T(2,128)S(1)}, f32[2,2,8,16,127]{4,1,0,3,2:T(2,128)}, u32[]{:S(2)}) copy-start(f32[2,2,8,16,127]{4,1,0,3,2:T(2,128)} %slice.554) | copy-start | bytes 780292
  42.1 3.5 %copy-start.6 = (f32[2,2,8,16,127]{4,1,0,3,2:T(2,128)S(1)}, f32[2,2,8,16,127]{4,1,0,3,2:T(2,128)}, u32[]{:S(2)}) copy-start(f32[2,2,8,16,127]{4,1,0,3,2:T(2,128)} %slice.556) | copy-start | bytes 780292
  42.1 3.5 %copy-start.7 = (f32[2,2,8,15,128]{4,1,0,3,2:T(2,128)S(1)}, f32[2,2,8,15,128]{4,1,0,3,2:T(2,128)}, u32[]{:S(2)}) copy-start(f32[2,2,8,15,128]{4,1,0,3,2:T(2,128)} %slice.547) | copy-start | bytes 737284
  42.1 3.5 %copy-start.8 = (f32[2,2,7,16,128]{4,1,0,3,2:T(2,128)S(1)}, f32[2,2,7,16,128]{4,1,0,3,2:T(2,128)}, u32[]{:S(2)}) copy-start(f32[2,2,7,16,128]{4,1,0,3,2:T(2,128)} %slice.557) | copy-start | bytes 688132
  47.5 10.7 %collective-permute-start.3 = (f32[2,2,2,16,128]{4,1,0,3,2:T(2,128)S(1)}, f32[2,2,2,16,128]{4,1,0,3,2:T(2,128)S(1)}, u32[]{:S(2)}, u32[]{:S(2)}) collective-permute-start(f32[2,2,2,16,128]{4,1,0,3,2:T(2,128)S(1)} %slice_bitcast_fusion.24), channel_id=1, source_target_pairs={{0,4},{4,8},{8,12},{12,16},{16,20},{20,24},{24,28},{28,32},{32,36}... | collective-permute-start | bytes 196616 | tf_op jit(solution)/shard_map/ppermute | solution.py:15
  50.1 7.9 %collective-permute-start.2 = (f32[2,2,2,8,128]{4,1,0,3,2:T(2,128)S(1)}, f32[2,2,2,8,128]{4,1,0,3,2:T(2,128)S(1)}, u32[]{:S(2)}, u32[]{:S(2)}) collective-permute-start(f32[2,2,2,8,128]{4,1,0,3,2:T(2,128)S(1)} %pad_maximum_fusion.2), channel_id=1, source_target_pairs={{0,1},{1,2},{2,3},{3,0},{4,5},{5,6},{6,7},{7,4},{8,9},{9,10},{10,1... | collective-permute-start | bytes 98312 | tf_op jit(solution)/shard_map/ppermute | solution.py:15
  61.9 7.1 %collective-permute-start.4 = (f32[2,2,2,8,128]{4,1,0,3,2:T(2,128)S(1)}, f32[2,2,2,8,128]{4,1,0,3,2:T(2,128)S(1)}, u32[]{:S(2)}, u32[]{:S(2)}) collective-permute-start(f32[2,2,2,8,128]{4,1,0,3,2:T(2,128)S(1)} %pad_maximum_fusion.3), channel_id=1, source_target_pairs={{0,3},{1,0},{2,1},{3,2},{4,7},{5,4},{6,5},{7,6},{8,11},{9,8},{10,9... | collective-permute-start | bytes 98312 | tf_op jit(solution)/shard_map/ppermute | solution.py:15
  64.6 6.5 %collective-permute-start.5 = (f32[2,2,2,16,128]{4,1,0,3,2:T(2,128)S(1)}, f32[2,2,2,16,128]{4,1,0,3,2:T(2,128)S(1)}, u32[]{:S(2)}, u32[]{:S(2)}) collective-permute-start(f32[2,2,2,16,128]{4,1,0,3,2:T(2,128)S(1)} %slice_bitcast_fusion.23), channel_id=1, source_target_pairs={{0,60},{4,0},{8,4},{12,8},{16,12},{20,16},{24,20},{28,24},{32,28},... | collective-permute-start | bytes 196616 | tf_op jit(solution)/shard_map/ppermute | solution.py:15
  74.2 10.0 %collective-permute-start.6 = (f32[2,2,2,8,128]{4,3,2,1,0:T(8,128)S(1)}, f32[2,2,2,8,128]{4,3,2,1,0:T(8,128)S(1)}, u32[]{:S(2)}, u32[]{:S(2)}) collective-permute-start(f32[2,2,2,8,128]{4,3,2,1,0:T(8,128)S(1)} %pad_maximum_fusion.4), channel_id=1, source_target_pairs={{0,1},{1,2},{2,3},{3,0},{4,5},{5,6},{6,7},{7,4},{8,9},{9,10},{10,1... | collective-permute-start | bytes 98312 | tf_op jit(solution)/shard_map/ppermute | solution.py:15
  79.0 7.1 %collective-permute-start.7 = (f32[2,2,2,16,128]{4,1,0,3,2:T(2,128)S(1)}, f32[2,2,2,16,128]{4,1,0,3,2:T(2,128)S(1)}, u32[]{:S(2)}, u32[]{:S(2)}) collective-permute-start(f32[2,2,2,16,128]{4,1,0,3,2:T(2,128)S(1)} %bitcast.365), channel_id=1, source_target_pairs={{0,4},{4,8},{8,12},{12,16},{16,20},{20,24},{24,28},{28,32},{32,36}... | collective-permute-start | bytes 196616 | tf_op jit(solution)/shard_map/ppermute | solution.py:15
  89.9 8.6 %collective-permute-start.8 = (f32[2,2,2,8,128]{4,1,0,3,2:T(2,128)S(1)}, f32[2,2,2,8,128]{4,1,0,3,2:T(2,128)S(1)}, u32[]{:S(2)}, u32[]{:S(2)}) collective-permute-start(f32[2,2,2,8,128]{4,1,0,3,2:T(2,128)S(1)} %pad_maximum_fusion.5), channel_id=1, source_target_pairs={{0,3},{1,0},{2,1},{3,2},{4,7},{5,4},{6,5},{7,6},{8,11},{9,8},{10,9... | collective-permute-start | bytes 98312 | tf_op jit(solution)/shard_map/ppermute | solution.py:15
  93.7 6.6 %collective-permute-start.9 = (f32[2,2,2,16,128]{4,1,0,3,2:T(2,128)S(1)}, f32[2,2,2,16,128]{4,1,0,3,2:T(2,128)S(1)}, u32[]{:S(2)}, u32[]{:S(2)}) collective-permute-start(f32[2,2,2,16,128]{4,1,0,3,2:T(2,128)S(1)} %slice_bitcast_fusion.22), channel_id=1, source_target_pairs={{0,60},{4,0},{8,4},{12,8},{16,12},{20,16},{24,20},{28,24},{32,28},... | collective-permute-start | bytes 196616 | tf_op jit(solution)/shard_map/ppermute | solution.py:15
  102.9 8.6 %collective-permute-start.10 = (f32[2,2,2,8,128]{4,3,2,1,0:T(8,128)S(1)}, f32[2,2,2,8,128]{4,3,2,1,0:T(8,128)S(1)}, u32[]{:S(2)}, u32[]{:S(2)}) collective-permute-start(f32[2,2,2,8,128]{4,3,2,1,0:T(8,128)S(1)} %copy.222), channel_id=1, source_target_pairs={{0,1},{1,2},{2,3},{3,0},{4,5},{5,6},{6,7},{7,4},{8,9},{9,10},{10,1... | collective-permute-start | bytes 98312 | tf_op jit(solution)/shard_map/ppermute | solution.py:15
  106.5 8.6 %collective-permute-start.11 = (f32[2,2,2,16,128]{4,1,0,3,2:T(2,128)S(1)}, f32[2,2,2,16,128]{4,1,0,3,2:T(2,128)S(1)}, u32[]{:S(2)}, u32[]{:S(2)}) collective-permute-start(f32[2,2,2,16,128]{4,1,0,3,2:T(2,128)S(1)} %bitcast.364), channel_id=1, source_target_pairs={{0,4},{4,8},{8,12},{12,16},{16,20},{20,24},{24,28},{28,32},{32,36}... | collective-permute-start | bytes 196616 | tf_op jit(solution)/shard_map/ppermute | solution.py:15
Sparse Core Ops, SparseCore 0:
  123.2 69.9 all-reduce.13
where the time goes:
time: 202 us
  waiting for transfers between devices  82.9 us (41%)
  starting transfers between devices  50.9 us (25%)
  other arithmetic  31.9 us (16%)
  between operations  18.5 us (9%)
  local copies, waits for them, and re-layouts  17.4 us (9%)
    psum x1, waiting for transfers between devices, shards(): whole = lax.psum(local_term, 'angle')  68.1 us
    ppermute x12, starting transfers between devices, from_behind(): return lax.ppermute(value, axis, pairs)  50.9 us
    ppermute x12, waiting for transfers between devices, from_behind(): return lax.ppermute(value, axis, pairs)  14.8 us
    sub x15, other arithmetic, rotate_runs(): real_part * cosine - imag_part * sine_full  5.45 us
    slice x6, local copies, waits for them, and re-layouts, next_depth(): field[..., 1:]  4.42 us
  transfers between devices with their start and end apart: 13, of which 6 were waited for; matrix products, arithmetic and copies ran while one was open for 11% of the time, Pallas kernels for 0%

commit v1 on v0

--- a/solution.py
+++ b/solution.py
@@ -121,7 +121,15 @@
     chosen = jnp.any(design_tiles == own_tile)
     local_term = jnp.where(chosen, local_term, jnp.zeros_like(local_term))
     groups = lax.axis_size("angle")
-    whole = lax.psum(local_term, "angle")
+    lanes = lax.psum(1, "angle")
+    whole, after = (local_term, 0)
+    while 1 << after < lanes:
+        row_list = []
+        for it in range(lanes):
+            row_list.append((it, it ^ 1 << after))
+        right_arr = lax.ppermute(whole, "angle", row_list)
+        whole = whole + right_arr
+        after = after + 1
     share = whole.shape[2] // groups
     summed = lax.dynamic_slice_in_dim(whole, lax.axis_index("angle") * share, share, 2)
     gradient = summed * (1.0 / groups)

time: 202 us -> 140 us (0.69)
  the two profiles are of different devices: /device:TPU:8 before, /device:TPU:6 now
where the time goes in v1:
time: 140 us; the launch traced here: 139 us
  starting transfers between devices  56.8 us (41%)
  other arithmetic  31.3 us (22%)
  waiting for transfers between devices  28.4 us (20%)
  local copies, waits for them, and re-layouts  17.4 us (12%)
  between operations  5.26 us (4%)
    ppermute x12, starting transfers between devices, from_behind(): return lax.ppermute(value, axis, pairs)  48.8 us
    ppermute x12, waiting for transfers between devices, from_behind(): return lax.ppermute(value, axis, pairs)  21.4 us
    ppermute x3, starting transfers between devices, shards(): right_arr = lax.ppermute(whole, 'angle', row_list)  7.97 us
    ppermute x3, waiting for transfers between devices, shards(): right_arr = lax.ppermute(whole, 'angle', row_list)  6.97 us
    sub x15, other arithmetic, rotate_runs(): real_part * cosine - imag_part * sine_full  5.45 us
    slice x6, local copies, waits for them, and re-layouts, next_depth(): field[..., 1:]  4.42 us
    add x3, other arithmetic, shards(): efield = efield + coef * curl_backward(hfield, phases)  3.17 us
  transfers between devices with their start and end apart: 15, of which 10 were waited for; matrix products, arithmetic and copies ran while one was open for 15% of the time, Pallas kernels for 0%

profile of v1, /device:TPU:6, one launch (start us, length us, event | category | flops | bytes accessed | tf_op | source)
XLA Modules:
  0.0 139.2 jit_solution(10067308921561425754)
XLA Ops:
  2.9 11.1 %collective-permute-start = (f32[2,2,2,8,128]{4,1,0,3,2:T(2,128)}, f32[2,2,2,8,128]{4,1,0,3,2:T(2,128)}, u32[]{:S(2)}, u32[]{:S(2)}) collective-permute-start(f32[2,2,2,8,128]{4,1,0,3,2:T(2,128)} %pad_maximum_fusion.1), channel_id=1, source_target_pairs={{0,3},{1,0},{2,1},{3,2},{4,7},{5,4},{6,5},{7,6},{8,11},{9,8},{10,9... | collective-permute-start | bytes 98312 | tf_op jit(solution)/shard_map/ppermute | solution.py:15
  15.2 6.3 %collective-permute-start.1 = (f32[2,2,2,16,128]{4,1,0,3,2:T(2,128)}, f32[2,2,2,16,128]{4,1,0,3,2:T(2,128)S(1)}, u32[]{:S(2)}, u32[]{:S(2)}) collective-permute-start(f32[2,2,2,16,128]{4,1,0,3,2:T(2,128)} %slice_bitcast_fusion.25), channel_id=1, source_target_pairs={{0,60},{4,0},{8,4},{12,8},{16,12},{20,16},{24,20},{28,24},{32,28},... | collective-permute-start | bytes 196616 | tf_op jit(solution)/shard_map/ppermute | solution.py:15
  32.4 2.0 %slice.554 = f32[2,2,8,16,127]{4,1,0,3,2:T(2,128)} slice(f32[2,2,8,16,128]{4,1,0,3,2:T(2,128)} %copy-done.4), slice={[0:2], [0:2], [0:8], [0:16], [1:128]} | slice | bytes 520192 | tf_op jit(solution)/shard_map/slice | solution.py:29
  44.2 1.9 %collective-permute-start.3 = (f32[2,2,2,16,128]{4,1,0,3,2:T(2,128)S(1)}, f32[2,2,2,16,128]{4,1,0,3,2:T(2,128)S(1)}, u32[]{:S(2)}, u32[]{:S(2)}) collective-permute-start(f32[2,2,2,16,128]{4,1,0,3,2:T(2,128)S(1)} %slice_bitcast_fusion.24), channel_id=1, source_target_pairs={{0,4},{4,8},{8,12},{12,16},{16,20},{20,24},{24,28},{28,32},{32,36}... | collective-permute-start | bytes 196616 | tf_op jit(solution)/shard_map/ppermute | solution.py:15
  46.1 1.9 %collective-permute-start.2 = (f32[2,2,2,8,128]{4,1,0,3,2:T(2,128)S(1)}, f32[2,2,2,8,128]{4,1,0,3,2:T(2,128)S(1)}, u32[]{:S(2)}, u32[]{:S(2)}) collective-permute-start(f32[2,2,2,8,128]{4,1,0,3,2:T(2,128)S(1)} %pad_maximum_fusion.2), channel_id=1, source_target_pairs={{0,1},{1,2},{2,3},{3,0},{4,5},{5,6},{6,7},{7,4},{8,9},{9,10},{10,1... | collective-permute-start | bytes 98312 | tf_op jit(solution)/shard_map/ppermute | solution.py:15
  48.1 5.9 %collective-permute-done.2 = f32[2,2,2,8,128]{4,1,0,3,2:T(2,128)S(1)} collective-permute-done((f32[2,2,2,8,128]{4,1,0,3,2:T(2,128)S(1)}, f32[2,2,2,8,128]{4,1,0,3,2:T(2,128)S(1)}, u32[]{:S(2)}, u32[]{:S(2)}) %collective-permute-start.2) | collective-permute-done | bytes 32800 | tf_op jit(solution)/shard_map/ppermute | solution.py:15
  57.9 1.9 %collective-permute-start.4 = (f32[2,2,2,8,128]{4,1,0,3,2:T(2,128)S(1)}, f32[2,2,2,8,128]{4,1,0,3,2:T(2,128)S(1)}, u32[]{:S(2)}, u32[]{:S(2)}) collective-permute-start(f32[2,2,2,8,128]{4,1,0,3,2:T(2,128)S(1)} %pad_maximum_fusion.3), channel_id=1, source_target_pairs={{0,3},{1,0},{2,1},{3,2},{4,7},{5,4},{6,5},{7,6},{8,11},{9,8},{10,9... | collective-permute-start | bytes 98312 | tf_op jit(solution)/shard_map/ppermute | solution.py:15
  60.6 6.2 %collective-permute-start.5 = (f32[2,2,2,16,128]{4,1,0,3,2:T(2,128)S(1)}, f32[2,2,2,16,128]{4,1,0,3,2:T(2,128)S(1)}, u32[]{:S(2)}, u32[]{:S(2)}) collective-permute-start(f32[2,2,2,16,128]{4,1,0,3,2:T(2,128)S(1)} %slice_bitcast_fusion.23), channel_id=1, source_target_pairs={{0,60},{4,0},{8,4},{12,8},{16,12},{20,16},{24,20},{28,24},{32,28},... | collective-permute-start | bytes 196616 | tf_op jit(solution)/shard_map/ppermute | solution.py:15
  71.6 4.8 %collective-permute-start.6 = (f32[2,2,2,8,128]{4,3,2,1,0:T(8,128)S(1)}, f32[2,2,2,8,128]{4,3,2,1,0:T(8,128)S(1)}, u32[]{:S(2)}, u32[]{:S(2)}) collective-permute-start(f32[2,2,2,8,128]{4,3,2,1,0:T(8,128)S(1)} %pad_maximum_fusion.4), channel_id=1, source_target_pairs={{0,1},{1,2},{2,3},{3,0},{4,5},{5,6},{6,7},{7,4},{8,9},{9,10},{10,1... | collective-permute-start | bytes 98312 | tf_op jit(solution)/shard_map/ppermute | solution.py:15
  76.4 1.9 %collective-permute-start.7 = (f32[2,2,2,16,128]{4,1,0,3,2:T(2,128)S(1)}, f32[2,2,2,16,128]{4,1,0,3,2:T(2,128)S(1)}, u32[]{:S(2)}, u32[]{:S(2)}) collective-permute-start(f32[2,2,2,16,128]{4,1,0,3,2:T(2,128)S(1)} %bitcast.365), channel_id=1, source_target_pairs={{0,4},{4,8},{8,12},{12,16},{16,20},{20,24},{24,28},{28,32},{32,36}... | collective-permute-start | bytes 196616 | tf_op jit(solution)/shard_map/ppermute | solution.py:15
  79.7 5.4 %collective-permute-done.7 = f32[2,2,2,16,128]{4,1,0,3,2:T(2,128)S(1)} collective-permute-done((f32[2,2,2,16,128]{4,1,0,3,2:T(2,128)S(1)}, f32[2,2,2,16,128]{4,1,0,3,2:T(2,128)S(1)}, u32[]{:S(2)}, u32[]{:S(2)}) %collective-permute-start.7) | collective-permute-done | bytes 65568 | tf_op jit(solution)/shard_map/ppermute | solution.py:15
  88.9 3.1 %collective-permute-start.8 = (f32[2,2,2,8,128]{4,1,0,3,2:T(2,128)S(1)}, f32[2,2,2,8,128]{4,1,0,3,2:T(2,128)S(1)}, u32[]{:S(2)}, u32[]{:S(2)}) collective-permute-start(f32[2,2,2,8,128]{4,1,0,3,2:T(2,128)S(1)} %pad_maximum_fusion.5), channel_id=1, source_target_pairs={{0,3},{1,0},{2,1},{3,2},{4,7},{5,4},{6,5},{7,6},{8,11},{9,8},{10,9... | collective-permute-start | bytes 98312 | tf_op jit(solution)/shard_map/ppermute | solution.py:15
  92.8 3.9 %collective-permute-start.9 = (f32[2,2,2,16,128]{4,1,0,3,2:T(2,128)S(1)}, f32[2,2,2,16,128]{4,1,0,3,2:T(2,128)S(1)}, u32[]{:S(2)}, u32[]{:S(2)}) collective-permute-start(f32[2,2,2,16,128]{4,1,0,3,2:T(2,128)S(1)} %slice_bitcast_fusion.22), channel_id=1, source_target_pairs={{0,60},{4,0},{8,4},{12,8},{16,12},{20,16},{24,20},{28,24},{32,28},... | collective-permute-start | bytes 196616 | tf_op jit(solution)/shard_map/ppermute | solution.py:15
  96.9 2.1 %collective-permute-done.9 = f32[2,2,2,16,128]{4,1,0,3,2:T(2,128)S(1)} collective-permute-done((f32[2,2,2,16,128]{4,1,0,3,2:T(2,128)S(1)}, f32[2,2,2,16,128]{4,1,0,3,2:T(2,128)S(1)}, u32[]{:S(2)}, u32[]{:S(2)}) %collective-permute-start.9) | collective-permute-done | bytes 65568 | tf_op jit(solution)/shard_map/ppermute | solution.py:15
  101.5 3.6 %collective-permute-start.10 = (f32[2,2,2,8,128]{4,3,2,1,0:T(8,128)S(1)}, f32[2,2,2,8,128]{4,3,2,1,0:T(8,128)S(1)}, u32[]{:S(2)}, u32[]{:S(2)}) collective-permute-start(f32[2,2,2,8,128]{4,3,2,1,0:T(8,128)S(1)} %copy.222), channel_id=1, source_target_pairs={{0,1},{1,2},{2,3},{3,0},{4,5},{5,6},{6,7},{7,4},{8,9},{9,10},{10,1... | collective-permute-start | bytes 98312 | tf_op jit(solution)/shard_map/ppermute | solution.py:15
  105.1 2.1 %collective-permute-start.11 = (f32[2,2,2,16,128]{4,1,0,3,2:T(2,128)S(1)}, f32[2,2,2,16,128]{4,1,0,3,2:T(2,128)S(1)}, u32[]{:S(2)}, u32[]{:S(2)}) collective-permute-start(f32[2,2,2,16,128]{4,1,0,3,2:T(2,128)S(1)} %bitcast.364), channel_id=1, source_target_pairs={{0,4},{4,8},{8,12},{12,16},{16,20},{20,24},{24,28},{28,32},{32,36}... | collective-permute-start | bytes 196616 | tf_op jit(solution)/shard_map/ppermute | solution.py:15
  107.6 1.8 %collective-permute-done.10 = f32[2,2,2,8,128]{4,3,2,1,0:T(8,128)S(1)} collective-permute-done((f32[2,2,2,8,128]{4,3,2,1,0:T(8,128)S(1)}, f32[2,2,2,8,128]{4,3,2,1,0:T(8,128)S(1)}, u32[]{:S(2)}, u32[]{:S(2)}) %collective-permute-start.10) | collective-permute-done | bytes 32800 | tf_op jit(solution)/shard_map/ppermute | solution.py:15
  109.5 3.8 %collective-permute-done.11 = f32[2,2,2,16,128]{4,1,0,3,2:T(2,128)S(1)} collective-permute-done((f32[2,2,2,16,128]{4,1,0,3,2:T(2,128)S(1)}, f32[2,2,2,16,128]{4,1,0,3,2:T(2,128)S(1)}, u32[]{:S(2)}, u32[]{:S(2)}) %collective-permute-start.11) | collective-permute-done | bytes 65568 | tf_op jit(solution)/shard_map/ppermute | solution.py:15
  117.1 2.4 %fusion.3 = f32[2,2,3,8,16,128]{5,1,0,4,2,3:T(2,128)S(1)} fusion(f32[2,1,3,8,16,128]{5,1,0,4,2,3:T(1,128)S(1)} %get-tuple-element.40, f32[2,1,3,8,16,128]{5,1,0,4,2,3:T(1,128)S(1)} %get-tuple-element.39, f32[2,1,3,8,16,128]{5,1,0,4,2,3:T(1,128)S(1)} %get-tuple-element.25, f32[2,1,3,8,16,128]{5,1,0,4,2,3:T(1,128)S(1)} %get-tuple-element.24, ...), kind=kLoop, calls=%fused_computation.7 | loop fusion | flops 1179648 | bytes 3932160 | tf_op jit(solution)/shard_map/add | solution.py:116
  120.8 1.9 %collective-permute-start.12 = (f32[8,16,128]{2,1,0:T(8,128)S(1)}, f32[8,16,128]{2,1,0:T(8,128)S(1)}, u32[]{:S(2)}, u32[]{:S(2)}) collective-permute-start(f32[8,16,128]{2,1,0:T(8,128)S(1)} %broadcast_select_fusion), channel_id=1, source_target_pairs={{0,64},{64,0},{128,192},{192,128},{256,320},{320,256},{384,448},{4... | collective-permute-start | bytes 196616 | tf_op jit(solution)/shard_map/ppermute | solution.py:130
  124.6 2.7 %collective-permute-start.13 = (f32[8,16,128]{2,1,0:T(8,128)S(1)}, f32[8,16,128]{2,1,0:T(8,128)S(1)}, u32[]{:S(2)}, u32[]{:S(2)}) collective-permute-start(f32[8,16,128]{2,1,0:T(8,128)S(1)} %fusion.65), channel_id=1, source_target_pairs={{0,128},{64,192},{128,0},{192,64},{256,384},{320,448},{384,256},{4... | collective-permute-start | bytes 196616 | tf_op jit(solution)/shard_map/ppermute | solution.py:130
  127.4 3.4 %collective-permute-done.13 = f32[8,16,128]{2,1,0:T(8,128)S(1)} collective-permute-done((f32[8,16,128]{2,1,0:T(8,128)S(1)}, f32[8,16,128]{2,1,0:T(8,128)S(1)}, u32[]{:S(2)}, u32[]{:S(2)}) %collective-permute-start.13) | collective-permute-done | bytes 65568 | tf_op jit(solution)/shard_map/ppermute | solution.py:130
  130.8 3.3 %collective-permute-start.14 = (f32[8,16,128]{2,1,0:T(8,128)S(1)}, f32[8,16,128]{2,1,0:T(8,128)S(1)}, u32[]{:S(2)}, u32[]{:S(2)}) collective-permute-start(f32[8,16,128]{2,1,0:T(8,128)S(1)} %add.140), channel_id=1, source_target_pairs={{0,256},{64,320},{128,384},{192,448},{256,0},{320,64},{384,128},{4... | collective-permute-start | bytes 196616 | tf_op jit(solution)/shard_map/ppermute | solution.py:130
  136.1 2.3 %collective-permute-done.14 = f32[8,16,128]{2,1,0:T(8,128)S(1)} collective-permute-done((f32[8,16,128]{2,1,0:T(8,128)S(1)}, f32[8,16,128]{2,1,0:T(8,128)S(1)}, u32[]{:S(2)}, u32[]{:S(2)}) %collective-permute-start.14) | collective-permute-done | bytes 65568 | tf_op jit(solution)/shard_map/ppermute | solution.py:130
  (173 shorter events, 48.0 us)
Async XLA Ops:
  2.9 19.4 %copy-start.10 = (f32[8,2]{0,1:T(2,128)S(1)}, f32[8,2]{0,1:T(2,128)}, u32[]{:S(2)}) copy-start(f32[8,2]{0,1:T(2,128)} %param.14) | copy-start | bytes 196
  2.9 36.0 %collective-permute-start = (f32[2,2,2,8,128]{4,1,0,3,2:T(2,128)}, f32[2,2,2,8,128]{4,1,0,3,2:T(2,128)}, u32[]{:S(2)}, u32[]{:S(2)}) collective-permute-start(f32[2,2,2,8,128]{4,1,0,3,2:T(2,128)} %pad_maximum_fusion.1), channel_id=1, source_target_pairs={{0,3},{1,0},{2,1},{3,2},{4,7},{5,4},{6,5},{7,6},{8,11},{9,8},{10,9... | collective-permute-start | bytes 98312 | tf_op jit(solution)/shard_map/ppermute | solution.py:15
  15.2 25.4 %collective-permute-start.1 = (f32[2,2,2,16,128]{4,1,0,3,2:T(2,128)}, f32[2,2,2,16,128]{4,1,0,3,2:T(2,128)S(1)}, u32[]{:S(2)}, u32[]{:S(2)}) collective-permute-start(f32[2,2,2,16,128]{4,1,0,3,2:T(2,128)} %slice_bitcast_fusion.25), channel_id=1, source_target_pairs={{0,60},{4,0},{8,4},{12,8},{16,12},{20,16},{24,20},{28,24},{32,28},... | collective-permute-start | bytes 196616 | tf_op jit(solution)/shard_map/ppermute | solution.py:15
  21.5 5.4 %copy-start = (f32[2,2,1,8,16,128]{5,4,3,2,1,0:T(8,128)}, f32[2,2,1,8,16,128]{5,4,3,2,1,0:T(8,128)S(1)}, u32[]{:S(2)}) copy-start(f32[2,2,1,8,16,128]{5,4,3,2,1,0:T(8,128)S(1)} %get-tuple-element.49) | copy-start | bytes 786436
  21.6 5.4 %copy-start.2 = (f32[2,2,8,16,128]{4,1,0,3,2:T(2,128)}, f32[2,2,8,16,128]{4,1,0,3,2:T(2,128)S(1)}, u32[]{:S(2)}) copy-start(f32[2,2,8,16,128]{4,1,0,3,2:T(2,128)S(1)} %slice_bitcast_fusion.21) | copy-start | bytes 786436
  32.4 5.3 %copy-start.3 = (f32[2,2,8,16,128]{4,1,0,3,2:T(2,128)S(1)}, f32[2,2,8,16,128]{4,1,0,3,2:T(2,128)}, u32[]{:S(2)}) copy-start(f32[2,2,8,16,128]{4,1,0,3,2:T(2,128)} %copy-done.2) | copy-start | bytes 786436
  38.8 3.5 %copy-start.1 = (f32[2,2,1,8,16,128]{5,4,3,2,1,0:T(8,128)S(1)}, f32[2,2,1,8,16,128]{5,4,3,2,1,0:T(8,128)}, u32[]{:S(2)}) copy-start(f32[2,2,1,8,16,128]{5,4,3,2,1,0:T(8,128)} %copy-done) | copy-start | bytes 786436
  38.8 3.5 %copy-start.5 = (f32[2,2,8,16,127]{4,1,0,3,2:T(2,128)S(1)}, f32[2,2,8,16,127]{4,1,0,3,2:T(2,128)}, u32[]{:S(2)}) copy-start(f32[2,2,8,16,127]{4,1,0,3,2:T(2,128)} %slice.554) | copy-start | bytes 780292
  38.8 3.5 %copy-start.6 = (f32[2,2,8,16,127]{4,1,0,3,2:T(2,128)S(1)}, f32[2,2,8,16,127]{4,1,0,3,2:T(2,128)}, u32[]{:S(2)}) copy-start(f32[2,2,8,16,127]{4,1,0,3,2:T(2,128)} %slice.556) | copy-start | bytes 780292
  38.8 3.5 %copy-start.7 = (f32[2,2,8,15,128]{4,1,0,3,2:T(2,128)S(1)}, f32[2,2,8,15,128]{4,1,0,3,2:T(2,128)}, u32[]{:S(2)}) copy-start(f32[2,2,8,15,128]{4,1,0,3,2:T(2,128)} %slice.547) | copy-start | bytes 737284
  38.8 3.5 %copy-start.8 = (f32[2,2,7,16,128]{4,1,0,3,2:T(2,128)S(1)}, f32[2,2,7,16,128]{4,1,0,3,2:T(2,128)}, u32[]{:S(2)}) copy-start(f32[2,2,7,16,128]{4,1,0,3,2:T(2,128)} %slice.557) | copy-start | bytes 688132
  44.2 10.0 %collective-permute-start.3 = (f32[2,2,2,16,128]{4,1,0,3,2:T(2,128)S(1)}, f32[2,2,2,16,128]{4,1,0,3,2:T(2,128)S(1)}, u32[]{:S(2)}, u32[]{:S(2)}) collective-permute-start(f32[2,2,2,16,128]{4,1,0,3,2:T(2,128)S(1)} %slice_bitcast_fusion.24), channel_id=1, source_target_pairs={{0,4},{4,8},{8,12},{12,16},{16,20},{20,24},{24,28},{28,32},{32,36}... | collective-permute-start | bytes 196616 | tf_op jit(solution)/shard_map/ppermute | solution.py:15
  46.1 7.9 %collective-permute-start.2 = (f32[2,2,2,8,128]{4,1,0,3,2:T(2,128)S(1)}, f32[2,2,2,8,128]{4,1,0,3,2:T(2,128)S(1)}, u32[]{:S(2)}, u32[]{:S(2)}) collective-permute-start(f32[2,2,2,8,128]{4,1,0,3,2:T(2,128)S(1)} %pad_maximum_fusion.2), channel_id=1, source_target_pairs={{0,1},{1,2},{2,3},{3,0},{4,5},{5,6},{6,7},{7,4},{8,9},{9,10},{10,1... | collective-permute-start | bytes 98312 | tf_op jit(solution)/shard_map/ppermute | solution.py:15
  57.9 8.9 %collective-permute-start.4 = (f32[2,2,2,8,128]{4,1,0,3,2:T(2,128)S(1)}, f32[2,2,2,8,128]{4,1,0,3,2:T(2,128)S(1)}, u32[]{:S(2)}, u32[]{:S(2)}) collective-permute-start(f32[2,2,2,8,128]{4,1,0,3,2:T(2,128)S(1)} %pad_maximum_fusion.3), channel_id=1, source_target_pairs={{0,3},{1,0},{2,1},{3,2},{4,7},{5,4},{6,5},{7,6},{8,11},{9,8},{10,9... | collective-permute-start | bytes 98312 | tf_op jit(solution)/shard_map/ppermute | solution.py:15
  60.6 7.9 %collective-permute-start.5 = (f32[2,2,2,16,128]{4,1,0,3,2:T(2,128)S(1)}, f32[2,2,2,16,128]{4,1,0,3,2:T(2,128)S(1)}, u32[]{:S(2)}, u32[]{:S(2)}) collective-permute-start(f32[2,2,2,16,128]{4,1,0,3,2:T(2,128)S(1)} %slice_bitcast_fusion.23), channel_id=1, source_target_pairs={{0,60},{4,0},{8,4},{12,8},{16,12},{20,16},{24,20},{28,24},{32,28},... | collective-permute-start | bytes 196616 | tf_op jit(solution)/shard_map/ppermute | solution.py:15
  71.6 7.9 %collective-permute-start.6 = (f32[2,2,2,8,128]{4,3,2,1,0:T(8,128)S(1)}, f32[2,2,2,8,128]{4,3,2,1,0:T(8,128)S(1)}, u32[]{:S(2)}, u32[]{:S(2)}) collective-permute-start(f32[2,2,2,8,128]{4,3,2,1,0:T(8,128)S(1)} %pad_maximum_fusion.4), channel_id=1, source_target_pairs={{0,1},{1,2},{2,3},{3,0},{4,5},{5,6},{6,7},{7,4},{8,9},{9,10},{10,1... | collective-permute-start | bytes 98312 | tf_op jit(solution)/shard_map/ppermute | solution.py:15
  76.4 8.6 %collective-permute-start.7 = (f32[2,2,2,16,128]{4,1,0,3,2:T(2,128)S(1)}, f32[2,2,2,16,128]{4,1,0,3,2:T(2,128)S(1)}, u32[]{:S(2)}, u32[]{:S(2)}) collective-permute-start(f32[2,2,2,16,128]{4,1,0,3,2:T(2,128)S(1)} %bitcast.365), channel_id=1, source_target_pairs={{0,4},{4,8},{8,12},{12,16},{16,20},{20,24},{24,28},{28,32},{32,36}... | collective-permute-start | bytes 196616 | tf_op jit(solution)/shard_map/ppermute | solution.py:15
  88.9 7.8 %collective-permute-start.8 = (f32[2,2,2,8,128]{4,1,0,3,2:T(2,128)S(1)}, f32[2,2,2,8,128]{4,1,0,3,2:T(2,128)S(1)}, u32[]{:S(2)}, u32[]{:S(2)}) collective-permute-start(f32[2,2,2,8,128]{4,1,0,3,2:T(2,128)S(1)} %pad_maximum_fusion.5), channel_id=1, source_target_pairs={{0,3},{1,0},{2,1},{3,2},{4,7},{5,4},{6,5},{7,6},{8,11},{9,8},{10,9... | collective-permute-start | bytes 98312 | tf_op jit(solution)/shard_map/ppermute | solution.py:15
  92.8 6.2 %collective-permute-start.9 = (f32[2,2,2,16,128]{4,1,0,3,2:T(2,128)S(1)}, f32[2,2,2,16,128]{4,1,0,3,2:T(2,128)S(1)}, u32[]{:S(2)}, u32[]{:S(2)}) collective-permute-start(f32[2,2,2,16,128]{4,1,0,3,2:T(2,128)S(1)} %slice_bitcast_fusion.22), channel_id=1, source_target_pairs={{0,60},{4,0},{8,4},{12,8},{16,12},{20,16},{24,20},{28,24},{32,28},... | collective-permute-start | bytes 196616 | tf_op jit(solution)/shard_map/ppermute | solution.py:15
  101.5 7.9 %collective-permute-start.10 = (f32[2,2,2,8,128]{4,3,2,1,0:T(8,128)S(1)}, f32[2,2,2,8,128]{4,3,2,1,0:T(8,128)S(1)}, u32[]{:S(2)}, u32[]{:S(2)}) collective-permute-start(f32[2,2,2,8,128]{4,3,2,1,0:T(8,128)S(1)} %copy.222), channel_id=1, source_target_pairs={{0,1},{1,2},{2,3},{3,0},{4,5},{5,6},{6,7},{7,4},{8,9},{9,10},{10,1... | collective-permute-start | bytes 98312 | tf_op jit(solution)/shard_map/ppermute | solution.py:15
  105.1 8.3 %collective-permute-start.11 = (f32[2,2,2,16,128]{4,1,0,3,2:T(2,128)S(1)}, f32[2,2,2,16,128]{4,1,0,3,2:T(2,128)S(1)}, u32[]{:S(2)}, u32[]{:S(2)}) collective-permute-start(f32[2,2,2,16,128]{4,1,0,3,2:T(2,128)S(1)} %bitcast.364), channel_id=1, source_target_pairs={{0,4},{4,8},{8,12},{12,16},{16,20},{20,24},{24,28},{28,32},{32,36}... | collective-permute-start | bytes 196616 | tf_op jit(solution)/shard_map/ppermute | solution.py:15
  120.8 3.1 %collective-permute-start.12 = (f32[8,16,128]{2,1,0:T(8,128)S(1)}, f32[8,16,128]{2,1,0:T(8,128)S(1)}, u32[]{:S(2)}, u32[]{:S(2)}) collective-permute-start(f32[8,16,128]{2,1,0:T(8,128)S(1)} %broadcast_select_fusion), channel_id=1, source_target_pairs={{0,64},{64,0},{128,192},{192,128},{256,320},{320,256},{384,448},{4... | collective-permute-start | bytes 196616 | tf_op jit(solution)/shard_map/ppermute | solution.py:130
  124.6 6.2 %collective-permute-start.13 = (f32[8,16,128]{2,1,0:T(8,128)S(1)}, f32[8,16,128]{2,1,0:T(8,128)S(1)}, u32[]{:S(2)}, u32[]{:S(2)}) collective-permute-start(f32[8,16,128]{2,1,0:T(8,128)S(1)} %fusion.65), channel_id=1, source_target_pairs={{0,128},{64,192},{128,0},{192,64},{256,384},{320,448},{384,256},{4... | collective-permute-start | bytes 196616 | tf_op jit(solution)/shard_map/ppermute | solution.py:130
  130.8 7.7 %collective-permute-start.14 = (f32[8,16,128]{2,1,0:T(8,128)S(1)}, f32[8,16,128]{2,1,0:T(8,128)S(1)}, u32[]{:S(2)}, u32[]{:S(2)}) collective-permute-start(f32[8,16,128]{2,1,0:T(8,128)S(1)} %add.140), channel_id=1, source_target_pairs={{0,256},{64,320},{128,384},{192,448},{256,0},{320,64},{384,128},{4... | collective-permute-start | bytes 196616 | tf_op jit(solution)/shard_map/ppermute | solution.py:130
  (2 other events, 2.9 us)
